TPU v7x, 256 devices: a whole 4x4x8 slice. The times are simulated.
256 devices in a mesh: dp: 32 (over y, z_hi, core), expert: 8 (over x, z_lo).
Axes of the slice: x: 4, y: 4, z: 8 (z_hi: 4, z_lo: 2; z = z_hi * 2 + z_lo), core: 2. Of those that a mesh axis runs over, the one named last changes fastest.
Arguments:
- tokens: bfloat16 [4096, 3072], P('dp', 'expert'), may hold values from -6 to 6
- out_grad: bfloat16 [4096, 3072], P('dp', 'expert'), may hold values from -6 to 6
- expert_ids: int32 [4096, 2], P('dp'), may hold values from 0 to 7, all different within a row; in each aligned block of 128 rows (0 to 127, 128 to 255, ...) at most 33 rows name the same one
- route_weights: float32 [4096, 2], P('dp'), may hold values from 0.2 to 1
- w_gate: bfloat16 [8, 3072, 8192], P('expert', None, 'dp'), may hold values from -0.109375 to 0.109375
- w_up: bfloat16 [8, 3072, 8192], P('expert', None, 'dp'), may hold values from -0.109375 to 0.109375
- w_down: bfloat16 [8, 8192, 3072], P('expert', 'dp'), may hold values from -0.0625 to 0.0625
Outputs:
- combined: bfloat16 [4096, 3072], P('dp', 'expert')
- d_gate: bfloat16 [8, 3072, 8192], P('expert', None, 'dp')
- d_up: bfloat16 [8, 3072, 8192], P('expert', None, 'dp')
- d_down: bfloat16 [8, 8192, 3072], P('expert', 'dp')
- d_route: float32 [4096, 2], P('dp')
Inputs may be any that keep to these rules, and one draw needn't show every extreme that they name: `expert_ids`: each token names 2 different experts; among the 128 tokens of one index of dp no expert is named more than 33 times, a bound that some block reaches.
All inputs are finite; a program needn't handle non-finite values.
Results may differ from a plain program's by a relative error of at most 0.02.
Values may be sent and summed in bfloat16 or wider, within the bound.
A program may use at most 128 MiB of HBM per device.

v0:
```python
import jax
import jax.numpy as jnp
from jax import lax
from jax.sharding import Mesh
from jax.sharding import PartitionSpec as P

highest = lax.Precision.HIGHEST
DP = ("dpo", "core")


def slot_table(routed, experts):
    flattened = routed.reshape(-1)
    onehot = (flattened[:, None] == jnp.arange(experts, dtype=jnp.int32)[None, :]).astype(jnp.int32)
    before = jnp.cumsum(onehot, axis=0) - onehot
    return jnp.sum(before * onehot, axis=1).reshape(routed.shape)


def pick_tables(routed, experts, capacity):
    places = slot_table(routed, experts)
    target = routed * capacity + places
    row_ids = jnp.arange(experts * capacity, dtype=jnp.int32)[:, None]
    return [
        (row_ids == target[None, :, which]).astype(jnp.float32) for which in range(routed.shape[1])
    ]


def local(tokens, out_grad, expert_ids, route_weights, w_gate, w_up, w_down):
    experts = lax.axis_size("expert")
    n_core = lax.axis_size("core")
    tok_rows, feat = tokens.shape
    top_count = expert_ids.shape[1]
    capacity = min(tok_rows, tok_rows * top_count * 33 // (32 * experts))
    picks = pick_tables(expert_ids, experts, capacity)
    dispatch = sum(picks)
    weighted = sum((picks[which] * route_weights[None, :, which] for which in range(top_count)))
    sent_tokens = jnp.dot(dispatch.astype(jnp.bfloat16), tokens, preferred_element_type=jnp.float32)
    sent_tokens = sent_tokens.astype(jnp.bfloat16).reshape(1, experts, capacity, feat)
    sent_grads = jnp.dot(weighted, out_grad.astype(jnp.float32), precision=highest)
    sent_grads = sent_grads.astype(jnp.bfloat16).reshape(1, experts, capacity, feat)
    sent_raw = jnp.dot(dispatch.astype(jnp.bfloat16), out_grad, preferred_element_type=jnp.float32)
    sent_raw = sent_raw.astype(jnp.bfloat16).reshape(1, experts, capacity, feat)
    sent = jnp.concatenate([sent_tokens, sent_grads, sent_raw], axis=0)
    recv = lax.all_to_all(sent, "expert", split_axis=1, concat_axis=3, tiled=True)
    both = jnp.concatenate([recv[0], recv[1]], axis=-1)
    blocks_all = lax.all_gather(both, DP, axis=0, tiled=True)
    n_blk = blocks_all.shape[0]
    d_all = recv.shape[-1]
    n_rows = n_blk * capacity
    flat_all = blocks_all.reshape(n_rows, 2 * d_all)
    gathered = flat_all[:, :d_all]
    grads_in = flat_all[:, d_all:]
    gate_slab = w_gate[0]
    up_slab = w_up[0]
    down_slab = w_down[0]
    gate_pre = jnp.dot(gathered, gate_slab, preferred_element_type=jnp.float32)
    up_pre = jnp.dot(gathered, up_slab, preferred_element_type=jnp.float32)
    sigmoid_gate = jax.nn.sigmoid(gate_pre)
    hidden = (gate_pre * sigmoid_gate * up_pre).astype(jnp.bfloat16)
    partial_out = jnp.dot(hidden, down_slab, preferred_element_type=jnp.float32).astype(
        jnp.bfloat16
    )
    d_hidden = jnp.einsum("rd,fd->rf", grads_in, down_slab, preferred_element_type=jnp.float32)
    d_down = jnp.einsum("rf,rd->fd", hidden, grads_in, preferred_element_type=jnp.float32).astype(
        jnp.bfloat16
    )
    d_gate_act = (
        d_hidden * up_pre * sigmoid_gate * (1.0 + gate_pre * (1.0 - sigmoid_gate))
    ).astype(jnp.bfloat16)
    d_up_act = (d_hidden * gate_pre * sigmoid_gate).astype(jnp.bfloat16)
    d_gate = jnp.einsum(
        "rd,rf->df", gathered, d_gate_act, preferred_element_type=jnp.float32
    ).astype(jnp.bfloat16)
    d_up = jnp.einsum("rd,rf->df", gathered, d_up_act, preferred_element_type=jnp.float32).astype(
        jnp.bfloat16
    )
    blocks = partial_out.reshape(n_blk, capacity, experts, d_all // experts).transpose(0, 2, 1, 3)
    summed_out = lax.psum_scatter(blocks, DP, scatter_dimension=0, tiled=True)
    raw_rows = recv[2, 0].reshape(capacity, experts, d_all // experts).astype(jnp.float32)
    dots = jnp.einsum("cfj,fcj->c", raw_rows, summed_out[0].astype(jnp.float32), precision=highest)
    hi = lax.reduce_precision(dots, exponent_bits=8, mantissa_bits=7)
    rest = dots - hi
    mid = lax.reduce_precision(rest, exponent_bits=8, mantissa_bits=7)
    lo = rest - mid
    pieces = jnp.stack([hi, mid, lo], axis=1).astype(jnp.bfloat16)
    lanes = jnp.pad(pieces, ((0, 0), (0, 128 - pieces.shape[1])))
    lanes = jnp.broadcast_to(lanes[None, None], (1, experts) + lanes.shape)
    payload = jnp.concatenate([summed_out, lanes], axis=-1)
    returned = lax.all_to_all(payload, "expert", split_axis=1, concat_axis=0, tiled=True)
    returned_out = returned[..., : d_all // experts]
    got = returned[..., d_all // experts : d_all // experts + 3].astype(jnp.float32)
    dots_all = (got[..., 0] + got[..., 1] + got[..., 2]).reshape(-1)
    flat_out = returned_out.reshape(experts * capacity, -1).astype(jnp.float32)
    combined = jnp.dot(weighted.T, flat_out, precision=highest).astype(jnp.bfloat16)
    target = expert_ids * capacity + slot_table(expert_ids, experts)
    d_route = dots_all[target]
    return (combined, d_gate[None], d_up[None], d_down[None], d_route)


def solution(mesh):
    n_dp, n_exp = mesh.devices.shape
    split = Mesh(mesh.devices.reshape(n_dp // 2, 2, n_exp), ("dpo", "core", "expert"))
    return jax.shard_map(
        local,
        mesh=split,
        in_specs=(
            P(DP, "expert"),
            P(DP, "expert"),
            P(DP, None),
            P(DP, None),
            P("expert", None, DP),
            P("expert", None, DP),
            P("expert", DP, None),
        ),
        out_specs=(
            P(DP, "expert"),
            P("expert", None, DP),
            P("expert", None, DP),
            P("expert", DP, None),
            P(DP, None),
        ),
        check_vma=False,
    )
```

profile of v0, /device:TPU:2, one launch (start us, length us, event | category | flops | bytes accessed | tf_op | source)
XLA Modules:
  0.0 306.3 jit_solution(1663517891706048601)
XLA Ops:
  7.2 0.9 copy.51
  8.4 0.6 reduce-window.6
  9.0 0.2 slice_reduce_fusion
  9.4 0.1 reshape.80
  9.6 0.7 compare_select_fusion
  10.3 1.1 convolution_convert_fusion.1
  11.5 0.8 slice_bitcast_fusion.3
  12.2 1.3 convolution_convert_fusion.2
  13.6 0.2 convolution_convert_fusion.3
  14.1 16.7 %all_to_all.27 = bf16[3,8,33,384]{3,2,0,1:T(8,128)(2,1)S(1)} all-to-all(bf16[3,8,33,384]{3,2,0,1:T(8,128)(2,1)S(1)} %copy.54), channel_id=1, replica_groups=mesh['dpo'=16,'core'=2,'expert'=8] {'expert'}, dimensions={1} | all-to-all | bytes 1216512 | tf_op jit(solution)/shard_map/all_to_all | solution.py:43
  31.2 0.8 pad_maximum_fusion.1
  32.1 106.2 %all-gather.2.cloned.1.call-done = bf16[32,33,6144]{2,1,0:T(8,128)(2,1)} async-done(((bf16[1,33,6144]{2,1,0:T(8,128)(2,1)}), bf16[32,33,6144]{2,1,0:T(8,128)(2,1)}) %all-gather.2.cloned.1.call-update) | async-done | bytes 12976144 | tf_op jit(solution)/shard_map/all_gather | solution.py:45
  138.3 11.8 %reshape.84 = bf16[1056,6144]{1,0:T(8,128)(2,1)} reshape(bf16[32,33,6144]{2,1,0:T(8,128)(2,1)} %all-gather.2.cloned.1.call-done) | data formatting | bytes 25952256 | tf_op jit(solution)/shard_map/reshape | solution.py:49
  150.1 5.3 %fusion.10 = f32[1056,256]{1,0:T(8,128)S(1)} fusion(bf16[1056,6144]{1,0:T(8,128)(2,1)} %reshape.84, bf16[1,3072,256]{2,1,0:T(8,128)(2,1)} %param.11), kind=kOutput, calls=%fused_computation.12 | convolution fusion | flops 1660944384 | bytes 9142272 | tf_op jit(solution)/shard_map/dot_general | solution.py:55
  155.4 1.7 copy-done.1
  157.1 0.4 copy-done.3
  157.5 2.9 multiply_convert_fusion.2
  160.4 1.9 convolution_convert_fusion
  162.3 4.4 %copy.67 = bf16[132,8,8,384]{3,2,1,0:T(8,128)(2,1)} copy(bf16[132,8,8,384]{3,1,2,0:T(8,128)(2,1)S(1)} %bitcast.71) | data formatting | bytes 12976128
  167.0 4.9 %fusion.2 = f32[1056,256]{1,0:T(8,128)S(1)} fusion(bf16[1056,6144]{1,0:T(8,128)(2,1)} %reshape.84, bf16[1,256,3072]{2,1,0:T(8,128)(2,1)S(1)} %copy-done), kind=kOutput, calls=%fused_computation.4 | convolution fusion | flops 1660944384 | bytes 9142272 | tf_op jit(solution)/shard_map/rd,fd->rf/dot_general | solution.py:62
  171.9 6.5 %fusion.24 = bf16[1,3072,256]{2,1,0:T(8,128)(2,1)} fusion(bf16[1056,6144]{1,0:T(8,128)(2,1)} %reshape.84, f32[1056,256]{1,0:T(8,128)S(1)} %fusion.2, f32[1056,256]{1,0:T(8,128)S(1)} %copy-done.5), kind=kOutput, calls=%fused_computation.18 | convolution fusion | flops 1663352832 | bytes 10223616 | tf_op jit(solution)/shard_map/rd,rf->df/dot_general | solution.py:73
  178.5 3.8 %fusion.27 = bf16[1,3072,256]{2,1,0:T(8,128)(2,1)} fusion(bf16[1056,6144]{1,0:T(8,128)(2,1)S(1)} %bitcast.74, f32[1056,256]{1,0:T(8,128)S(1)} %copy-done.5, f32[1056,256]{1,0:T(8,128)S(1)} %fusion.2, f32[1056,256]{1,0:T(8,128)S(1)} %copy-done.6), kind=kOutput, calls=%fused_computation.19 | convolution fusion | flops 1664434176 | bytes 11304960 | tf_op jit(solution)/shard_map/rd,rf->df/dot_general | solution.py:70
  182.3 98.7 %reduce-scatter.4.cloned.1.call-done = bf16[1,8,33,384]{3,1,2,0:T(8,128)(2,1)} async-done(((bf16[32,8,33,384]{3,1,2,0:T(8,128)(2,1)}), bf16[1,8,33,384]{3,1,2,0:T(8,128)(2,1)}) %reduce-scatter.4.cloned.1.call-update) | async-done | bytes 202768
  281.0 1.3 multiply_reduce_fusion
  282.4 1.0 pad_maximum_fusion.2
  283.4 0.8 copy.58
  284.2 4.8 %all-to-all-start.1 = ((bf16[1,8,33,512]{3,2,0,1:T(8,128)(2,1)}), bf16[1,8,33,512]{3,2,0,1:T(8,128)(2,1)S(1)}, u32[]{:S(2)}, u32[]{:S(2)}) async-start(bf16[1,8,33,512]{3,2,0,1:T(8,128)(2,1)} %copy.58), calls=%async_computation.1 | async-start | bytes 655360 | tf_op jit(solution)/shard_map/all_to_all | solution.py:88
  289.0 6.3 %fusion.21 = bf16[1,256,3072]{2,1,0:T(8,128)(2,1)} fusion(bf16[1056,256]{1,0:T(8,128)(2,1)S(1)} %get-tuple-element.42, bf16[1056,6144]{1,0:T(8,128)(2,1)} %reshape.84), kind=kOutput, calls=%fused_computation.17 | convolution fusion | flops 1661730816 | bytes 8601600 | tf_op jit(solution)/shard_map/rf,rd->fd/dot_general | solution.py:63
  295.4 1.1 convolution_convert_fusion.4
  296.5 0.2 fusion.37
  296.8 2.0 gather_fusion
  298.9 0.6 copy.60
  (57 shorter events, 2.2 us)
Async XLA Ops:
  7.2 153.3 %copy-start = (bf16[1,256,3072]{2,1,0:T(8,128)(2,1)S(1)}, bf16[1,256,3072]{2,1,0:T(8,128)(2,1)}, u32[]{:S(2)}) copy-start(bf16[1,256,3072]{2,1,0:T(8,128)(2,1)} %param.13) | copy-start | bytes 4718596
  7.2 6.4 %copy-start.2 = (bf16[128,384]{1,0:T(8,128)(2,1)S(1)}, bf16[128,384]{1,0:T(8,128)(2,1)}, u32[]{:S(2)}) copy-start(bf16[128,384]{1,0:T(8,128)(2,1)} %param.7) | copy-start | bytes 294916
  7.2 131.1 %all-gather.2.cloned.1.call-start = ((), (), s32[]{:S(2)}) async-start(), calls=%async_computation.3 | async-start | bytes 16220160 | tf_op jit(solution)/shard_map/all_gather | solution.py:45
  32.0 248.9 %reduce-scatter.4.cloned.1.call-start = ((), (), s32[]{:S(2)}) async-start(), calls=%async_computation.4 | async-start | bytes 6690816
  150.1 7.0 %copy-start.1 = (bf16[1056,6144]{1,0:T(8,128)(2,1)S(1)}, bf16[1056,6144]{1,0:T(8,128)(2,1)}, u32[]{:S(2)}) copy-start(bf16[1056,6144]{1,0:T(8,128)(2,1)} %reshape.84) | copy-start | bytes 38928388
  150.1 7.4 %copy-start.3 = (bf16[1,3072,256]{2,1,0:T(8,128)(2,1)S(1)}, bf16[1,3072,256]{2,1,0:T(8,128)(2,1)}, u32[]{:S(2)}) copy-start(bf16[1,3072,256]{2,1,0:T(8,128)(2,1)} %param.12) | copy-start | bytes 4718596
  157.5 2.9 copy-start.4
  167.0 4.9 %copy-start.5 = (f32[1056,256]{1,0:T(8,128)S(1)}, f32[1056,256]{1,0:T(8,128)}, u32[]{:S(2)}) copy-start(f32[1056,256]{1,0:T(8,128)} %copy-done.4) | copy-start | bytes 3244036
  167.0 11.5 %slice-start = ((s8[12976128]{0:T(1024)(128)(4,1)}), s8[4194304]{0:T(1024)(128)(4,1)S(1)}, s32[]{:S(2)}) async-start(s8[12976128]{0:T(1024)(128)(4,1)} %bitcast.73), calls=%async_computation.5 | async-start | bytes 8388608
  167.0 11.5 %slice-start.1 = ((s8[12976128]{0:T(1024)(128)(4,1)}), s8[4194304]{0:T(1024)(128)(4,1)S(1)}, s32[]{:S(2)}) async-start(s8[12976128]{0:T(1024)(128)(4,1)} %bitcast.73), calls=%async_computation.6 | async-start | bytes 8388608
  171.9 6.6 %slice-start.2 = ((s8[12976128]{0:T(1024)(128)(4,1)}), s8[4194304]{0:T(1024)(128)(4,1)S(1)}, s32[]{:S(2)}) async-start(s8[12976128]{0:T(1024)(128)(4,1)} %bitcast.73), calls=%async_computation.7 | async-start | bytes 8388608
  171.9 6.6 %slice-start.3 = ((s8[12976128]{0:T(1024)(128)(4,1)}), s8[393216]{0:T(1024)(128)(4,1)S(1)}, s32[]{:S(2)}) async-start(s8[12976128]{0:T(1024)(128)(4,1)} %bitcast.73), calls=%async_computation.8 | async-start | bytes 786432
  171.9 6.5 %copy-start.6 = (f32[1056,256]{1,0:T(8,128)S(1)}, f32[1056,256]{1,0:T(8,128)}, u32[]{:S(2)}) copy-start(f32[1056,256]{1,0:T(8,128)} %get-tuple-element.43) | copy-start | bytes 3244036
  284.2 11.1 %all-to-all-start.1 = ((bf16[1,8,33,512]{3,2,0,1:T(8,128)(2,1)}), bf16[1,8,33,512]{3,2,0,1:T(8,128)(2,1)S(1)}, u32[]{:S(2)}, u32[]{:S(2)}) async-start(bf16[1,8,33,512]{3,2,0,1:T(8,128)(2,1)} %copy.58), calls=%async_computation.1 | async-start | bytes 655360 | tf_op jit(solution)/shard_map/all_to_all | solution.py:88
Sparse Core Ops, SparseCore 0:
  32.2 106.0 all-gather.1
  166.8 114.1 reduce-scatter.3
where the time goes:
time: 307 us; the launch traced here: 306 us
  waiting for transfers between devices  205 us (67%)
  matrix products  35.2 us (11%)
  local copies, waits for them, and re-layouts  25.4 us (8%)
  blocking collectives  16.7 us (5%)
  between operations  14.4 us (5%)
  other arithmetic  4.92 us (2%)
  starting transfers between devices  4.86 us (2%)
    all_gather x1, waiting for transfers between devices, local(): blocks_all = lax.all_gather(both, DP, axis=0, tiled=True)  106 us
    unnamed x3, waiting for transfers between devices  98.7 us
    all_to_all x1, blocking collectives, local(): lax.all_to_all(sent, 'expert', split_axis=1, concat_axis=3, tiled=True)  16.7 us
    reshape x1, local copies, waits for them, and re-layouts, local(): flat_all = blocks_all.reshape(n_rows, 2 * d_all)  11.8 us
    unnamed x26, local copies, waits for them, and re-layouts  8.19 us
    dot_general x1, matrix products, local(): jnp.einsum('rd,rf->df', gathered, d_up_act, preferred_element_type=jnp.fl...  6.51 us
    dot_general x1, matrix products, local(): jnp.einsum('rf,rd->fd', hidden, grads_in, preferred_element_type=jnp.floa...  6.28 us
  transfers between devices with their start and end apart: 3, of which 2 were waited for; matrix products, arithmetic and copies ran while one was open for 7% of the time, Pallas kernels for 0%

commit v1 on v0

--- a/solution.py
+++ b/solution.py
@@ -42,7 +42,9 @@
     sent = jnp.concatenate([sent_tokens, sent_grads, sent_raw], axis=0)
     recv = lax.all_to_all(sent, "expert", split_axis=1, concat_axis=3, tiled=True)
     both = jnp.concatenate([recv[0], recv[1]], axis=-1)
-    blocks_all = lax.all_gather(both, DP, axis=0, tiled=True)
+    blocks_all = jnp.concatenate(
+        lax.all_to_all(jnp.stack([both] * lax.axis_size(DP)), DP, 0, 0), axis=0
+    )
     n_blk = blocks_all.shape[0]
     d_all = recv.shape[-1]
     n_rows = n_blk * capacity

time: 307 us -> 545 us (1.78)
  blocking collectives: 16.7 us -> 355 us
  waiting for transfers between devices: 205 us -> 103 us
    all_to_all x0 -> x1, blocking collectives: none -> 339 us  [local(): lax.all_to_all(jnp.stack([both] * lax.axis_size(DP)), DP, 0, 0)]
    all_gather x1 -> x0, waiting for transfers between devices: 106 us -> none  [local(): blocks_all = lax.all_gather(both, DP, axis=0, tiled=True)]
    another operation x1 -> x3, local copies, waits for them, and re-layouts: 0.01 us -> 13.8 us  [the longest x1 11.8 us: local(): flat_all = blocks_all.reshape(n_rows, 2 * d_all)]
    reshape x1 -> x0, local copies, waits for them, and re-layouts: 11.8 us -> none  [local(): flat_all = blocks_all.reshape(n_rows, 2 * d_all)]
    unnamed x3 -> x2, waiting for transfers between devices: 98.7 us -> 103 us
  transfers between devices with their start and end apart: 3 -> 2, of which waited for: 2 -> 1; matrix products, arithmetic and copies ran while one was open for 7% -> 4% of each run, Pallas kernels for 0% -> 0%
where the time goes in v1:
time: 545 us
  blocking collectives  355 us (65%)
  waiting for transfers between devices  103 us (19%)
  matrix products  35.3 us (6%)
  local copies, waits for them, and re-layouts  27.4 us (5%)
  between operations  14.4 us (3%)
    all_to_all x1, blocking collectives, local(): lax.all_to_all(jnp.stack([both] * lax.axis_size(DP)), DP, 0, 0)  339 us
    unnamed x2, waiting for transfers between devices  103 us
    all_to_all x1, blocking collectives, local(): lax.all_to_all(sent, 'expert', split_axis=1, concat_axis=3, tiled=True)  16.7 us
    another operation x1, local copies, waits for them, and re-layouts, local(): flat_all = blocks_all.reshape(n_rows, 2 * d_all)  11.8 us
  transfers between devices with their start and end apart: 2, of which 1 were waited for; matrix products, arithmetic and copies ran while one was open for 4% of the time, Pallas kernels for 0%

profile of v1, /device:TPU:2, one launch (start us, length us, event | category | flops | bytes accessed | tf_op | source)
XLA Modules:
  0.0 544.7 jit_solution(12827543385427312132)
XLA Ops:
  7.2 0.9 copy.51
  8.4 0.6 reduce-window.6
  9.0 0.2 slice_reduce_fusion
  9.4 0.1 reshape.80
  9.6 0.7 compare_select_fusion
  10.3 1.1 convolution_convert_fusion.1
  11.5 0.8 slice_bitcast_fusion.3
  12.2 1.3 convolution_convert_fusion.2
  13.6 0.2 convolution_convert_fusion.3
  14.1 16.7 %all_to_all.32 = bf16[3,8,33,384]{3,2,0,1:T(8,128)(2,1)S(1)} all-to-all(bf16[3,8,33,384]{3,2,0,1:T(8,128)(2,1)S(1)} %copy.54), channel_id=1, replica_groups=mesh['dpo'=16,'core'=2,'expert'=8] {'expert'}, dimensions={1} | all-to-all | bytes 1216512 | tf_op jit(solution)/shard_map/all_to_all | solution.py:43
  31.2 2.0 stack.14
  33.3 338.8 %all_to_all.33 = bf16[32,1,33,6144]{3,2,1,0:T(8,128)(2,1)} all-to-all(bf16[32,1,33,6144]{3,2,1,0:T(8,128)(2,1)S(1)} %stack.14), channel_id=1, replica_groups=mesh['dpo'=16,'core'=2,'expert'=8] {'dpo','core'}, dimensions={0} | all-to-all | bytes 25952256 | tf_op jit(solution)/shard_map/all_to_all | solution.py:46
  372.1 11.8 %reshape_reshape.3 = bf16[1056,6144]{1,0:T(8,128)(2,1)} reshape(bf16[32,1,33,6144]{3,2,1,0:T(8,128)(2,1)} %all_to_all.33) | data formatting | bytes 25952256 | tf_op jit(solution)/shard_map/reshape;reshape | solution.py:51
  383.9 5.3 fusion.10
  389.2 1.7 copy-done.2
  390.9 0.4 copy-done.4
  391.3 2.9 multiply_convert_fusion.2
  394.2 1.9 convolution_convert_fusion
  396.0 4.4 copy.67
  400.7 4.9 fusion.2
  405.6 6.6 %fusion.24 = bf16[1,3072,256]{2,1,0:T(8,128)(2,1)} fusion(bf16[1056,6144]{1,0:T(8,128)(2,1)} %reshape_reshape.3, f32[1056,256]{1,0:T(8,128)S(1)} %fusion.2, f32[1056,256]{1,0:T(8,128)S(1)} %copy-done.6), kind=kOutput, calls=%fused_computation.18 | convolution fusion | flops 1663352832 | bytes 10223616 | tf_op jit(solution)/shard_map/rd,rf->df/dot_general | solution.py:75
  412.3 4.0 fusion.27
  416.3 103.0 %reduce-scatter.4.cloned.1.call-done = bf16[1,8,33,384]{3,1,2,0:T(8,128)(2,1)} async-done(((bf16[32,8,33,384]{3,1,2,0:T(8,128)(2,1)}), bf16[1,8,33,384]{3,1,2,0:T(8,128)(2,1)}) %reduce-scatter.4.cloned.1.call-update) | async-done | bytes 202768
  519.3 1.3 multiply_reduce_fusion
  520.7 1.0 pad_maximum_fusion.1
  521.7 0.8 copy.58
  522.5 4.8 all-to-all-start.2
  527.3 6.2 %fusion.21 = bf16[1,256,3072]{2,1,0:T(8,128)(2,1)} fusion(bf16[1056,256]{1,0:T(8,128)(2,1)S(1)} %get-tuple-element.42, bf16[1056,6144]{1,0:T(8,128)(2,1)} %reshape_reshape.3), kind=kOutput, calls=%fused_computation.17 | convolution fusion | flops 1661730816 | bytes 8601600 | tf_op jit(solution)/shard_map/rf,rd->fd/dot_general | solution.py:65
  533.7 1.1 convolution_convert_fusion.4
  534.8 0.2 fusion.37
  535.1 2.0 gather_fusion
  537.2 0.6 copy.60
  (58 shorter events, 2.1 us)
Async XLA Ops:
  7.2 387.0 %copy-start = (bf16[1,256,3072]{2,1,0:T(8,128)(2,1)S(1)}, bf16[1,256,3072]{2,1,0:T(8,128)(2,1)}, u32[]{:S(2)}) copy-start(bf16[1,256,3072]{2,1,0:T(8,128)(2,1)} %param.13) | copy-start | bytes 4718596
  7.2 6.4 %copy-start.3 = (bf16[128,384]{1,0:T(8,128)(2,1)S(1)}, bf16[128,384]{1,0:T(8,128)(2,1)}, u32[]{:S(2)}) copy-start(bf16[128,384]{1,0:T(8,128)(2,1)} %param.7) | copy-start | bytes 294916
  7.2 512.1 %reduce-scatter.4.cloned.1.call-start = ((), (), s32[]{:S(2)}) async-start(), calls=%async_computation.4 | async-start | bytes 6690816
  383.9 7.0 %copy-start.2 = (bf16[1056,6144]{1,0:T(8,128)(2,1)S(1)}, bf16[1056,6144]{1,0:T(8,128)(2,1)}, u32[]{:S(2)}) copy-start(bf16[1056,6144]{1,0:T(8,128)(2,1)} %reshape_reshape.3) | copy-start | bytes 38928388
  383.9 7.4 %copy-start.4 = (bf16[1,3072,256]{2,1,0:T(8,128)(2,1)S(1)}, bf16[1,3072,256]{2,1,0:T(8,128)(2,1)}, u32[]{:S(2)}) copy-start(bf16[1,3072,256]{2,1,0:T(8,128)(2,1)} %param.12) | copy-start | bytes 4718596
  391.3 2.9 copy-start.5
  400.7 4.9 copy-start.6
  400.7 11.5 %slice-start = ((s8[12976128]{0:T(1024)(128)(4,1)}), s8[4194304]{0:T(1024)(128)(4,1)S(1)}, s32[]{:S(2)}) async-start(s8[12976128]{0:T(1024)(128)(4,1)} %bitcast.75), calls=%async_computation.5 | async-start | bytes 8388608
  400.7 11.5 %slice-start.1 = ((s8[12976128]{0:T(1024)(128)(4,1)}), s8[4194304]{0:T(1024)(128)(4,1)S(1)}, s32[]{:S(2)}) async-start(s8[12976128]{0:T(1024)(128)(4,1)} %bitcast.75), calls=%async_computation.6 | async-start | bytes 8388608
  405.6 6.6 %slice-start.2 = ((s8[12976128]{0:T(1024)(128)(4,1)}), s8[4194304]{0:T(1024)(128)(4,1)S(1)}, s32[]{:S(2)}) async-start(s8[12976128]{0:T(1024)(128)(4,1)} %bitcast.75), calls=%async_computation.7 | async-start | bytes 8388608
  405.6 6.6 %slice-start.3 = ((s8[12976128]{0:T(1024)(128)(4,1)}), s8[393216]{0:T(1024)(128)(4,1)S(1)}, s32[]{:S(2)}) async-start(s8[12976128]{0:T(1024)(128)(4,1)} %bitcast.75), calls=%async_computation.8 | async-start | bytes 786432
  405.6 6.6 %copy-start.7 = (f32[1056,256]{1,0:T(8,128)S(1)}, f32[1056,256]{1,0:T(8,128)}, u32[]{:S(2)}) copy-start(f32[1056,256]{1,0:T(8,128)} %get-tuple-element.43) | copy-start | bytes 3244036
  522.5 11.1 %all-to-all-start.2 = ((bf16[1,8,33,512]{3,2,0,1:T(8,128)(2,1)}), bf16[1,8,33,512]{3,2,0,1:T(8,128)(2,1)S(1)}, u32[]{:S(2)}, u32[]{:S(2)}) async-start(bf16[1,8,33,512]{3,2,0,1:T(8,128)(2,1)} %copy.58), calls=%async_computation.2 | async-start | bytes 655360 | tf_op jit(solution)/shard_map/all_to_all | solution.py:90
  535.1 2.7 copy-start.1
Sparse Core Ops, SparseCore 0:
  400.5 118.6 reduce-scatter.3
